TPU v7x, 512 devices: a whole 4x8x8 slice. The times are simulated.
512 devices in a mesh: seq: 128 (over z, y, core), tp: 4 (over x).
Axes of the slice: x: 4, y: 8, z: 8, core: 2. Of those that a mesh axis runs over, the one named last changes fastest.
Arguments:
- tokens: bfloat16 [32768, 1536], P('seq', 'tp'), may hold values from -6 to 6
- norm_gain: float32 [1536], replicated, may hold values from 0.1 to 1.9
- query_weight: bfloat16 [1536, 1536], P(None, 'tp'), may hold values from -0.15625 to 0.15625
- query_bias: float32 [1536], P('tp'), may hold values from -10 to 10
- kv_weight: bfloat16 [1536, 512], P(None, 'tp'), may hold values from -0.15625 to 0.15625
- kv_bias: float32 [512], P('tp'), may hold values from -3 to 3
- out_weight: bfloat16 [1536, 1536], P('tp'), may hold values from -0.625 to 0.625
- shared_slot: bfloat16 [32768, 512], P('seq'), may hold values from -6 to 6
- shared_len: int32 [5], replicated, may hold values from 1 to 256, as said below
- shared_owner: int32 [5], replicated, may hold values from 0 to 127, as said below
- hist_pool: bfloat16 [2048, 64, 512], P('seq'), may hold values from -6 to 6
- hist_pages: int32 [128, 16], P('seq'), may hold values from 0 to 15, each once within a row
- hist_len: int32 [128, 4], P('seq'), may hold values from 1 to 256, as said below
- req_len: int32 [128, 4], P('seq'), may hold values from 1 to 128, 256 in all within a row
- req_offset: int32 [128, 4], P('seq'), may hold values from 0 to 3, each once within a row
- req_parent: int32 [128, 4], P('seq'), may hold values from 0 to 3
Outputs:
- hidden: bfloat16 [32768, 1536], P('seq', 'tp')
- new_cache: bfloat16 [32768, 512], P('seq', 'tp')
Inputs may be any that keep to these rules, and one draw needn't show every extreme that they name: `shared_owner`: all different; entry 0 is the root's. `shared_len`: some entry equals 256. `hist_len`: some request's history has exactly 256 rows.
All inputs are finite; a program needn't handle non-finite values.
Results may differ from a plain program's by a relative error of at most 0.017.
Values may be sent and summed in bfloat16 or wider, within the bound.
No kernel may reach another device: no remote copies, remote signals or barrier semaphores. Data moves between devices by JAX's collectives and lax.ppermute only.
A program may use at most 64 MiB of HBM per device.

v0:
```python
import jax
import jax.numpy as jnp
from jax import lax
from jax.sharding import PartitionSpec as P

norm_eps = 1e-06
rope_base = 1000000.0
neighbour_steps = (-2, -1, 1, 2)
masked_score = -1e30


def from_partner(shard, axis, apart):
    return lax.ppermute(shard, axis, [(i, i ^ 1 << apart) for i in range(lax.axis_size(axis))])


def spread(shard, axis, root):
    mine = lax.axis_index(axis) == root
    return lax.psum(jnp.where(mine, shard, jnp.zeros_like(shard)), axis)


def passed_along(block, axis, distance):
    devices = range(lax.axis_size(axis))
    route = [((i - distance) % len(devices), i) for i in devices]
    return lax.ppermute(block, axis, route)


def request_layout(req_len, req_parent, hist_len, shared_len, row_count):
    request_end = jnp.cumsum(req_len, axis=1)
    request_start = request_end - req_len
    row_index = jnp.arange(row_count, dtype=jnp.int32)
    row_request = jnp.sum(
        (row_index[None, :, None] >= request_end[:, None, :]).astype(jnp.int32), axis=2
    )
    slot_numbers = jnp.arange(req_len.shape[1], dtype=jnp.int32)
    chosen = row_request[:, :, None] == slot_numbers[None, None, :]

    def lookup(table):
        return jnp.sum(jnp.where(chosen, table[:, None, :], 0), axis=2)

    row_offset = row_index[None, :] - lookup(request_start)
    row_parent = lookup(req_parent)
    node_numbers = jnp.arange(shared_len.shape[0] - 1, dtype=jnp.int32)
    parent_length = jnp.sum(
        jnp.where(row_parent[:, :, None] == node_numbers, shared_len[1:], 0), axis=2
    )
    position = shared_len[0] + parent_length + lookup(hist_len) + row_offset
    return (row_request, row_parent, position)


def rotate(values, position):
    half_dim = values.shape[-1] // 2
    frequency = rope_base ** (-2.0 * jnp.arange(half_dim, dtype=jnp.float32) / values.shape[-1])
    angle = position.astype(jnp.float32)[:, None, None] * frequency
    cosine = jnp.cos(angle)
    sine = jnp.sin(angle)
    first_half = values[..., :half_dim]
    second_half = values[..., half_dim:]
    return jnp.concatenate(
        [first_half * cosine - second_half * sine, second_half * cosine + first_half * sine],
        axis=-1,
    )


def partial_attention(queries, key_vectors, value_vectors, key_mask):
    score_scale = queries.shape[-1] ** (-0.5)
    scores = (
        jnp.einsum("rhd,kd->rhk", queries, key_vectors, preferred_element_type=jnp.float32)
        * score_scale
    )
    scores = jnp.where(key_mask[:, None, :], scores, masked_score)
    top_score = jnp.max(scores, axis=2)
    weights = jnp.where(key_mask[:, None, :], jnp.exp(scores - top_score[:, :, None]), 0.0)
    weight_sum = jnp.sum(weights, axis=2)
    mixed = jnp.einsum(
        "rhk,kd->rhd",
        weights.astype(jnp.bfloat16),
        value_vectors,
        preferred_element_type=jnp.float32,
    )
    return (top_score, weight_sum, mixed)


def combine(first_part, second_part):
    top_score = jnp.maximum(first_part[0], second_part[0])
    first_scale = jnp.exp(first_part[0] - top_score)
    second_scale = jnp.exp(second_part[0] - top_score)
    weight_sum = first_part[1] * first_scale + second_part[1] * second_scale
    mixed = first_part[2] * first_scale[:, :, None] + second_part[2] * second_scale[:, :, None]
    return (top_score, weight_sum, mixed)


def on_device(
    tokens,
    norm_gain,
    query_weight,
    query_bias,
    kv_weight,
    kv_bias,
    out_weight,
    shared_slot,
    shared_len,
    shared_owner,
    hist_pool,
    hist_pages,
    hist_len,
    req_len,
    req_offset,
    req_parent,
):
    features = lax.all_gather(tokens, "tp", axis=1, tiled=True)
    widened = features.astype(jnp.float32)
    mean_square = jnp.mean(widened * widened, axis=1, keepdims=True)
    normed = (widened * lax.rsqrt(mean_square + norm_eps) * norm_gain).astype(jnp.bfloat16)
    head_dim = kv_bias.shape[0]
    head_count = query_weight.shape[1] // head_dim
    row_count = features.shape[0]
    tp_index = lax.axis_index("tp")
    kv_group = tp_index // 2
    holds_key = tp_index % 2 == 0
    row_request, row_parent, position = request_layout(
        req_len, req_parent, hist_len, shared_len, row_count
    )
    row_request = row_request[0]
    row_parent = row_parent[0]
    position = position[0]
    queries = jnp.dot(normed, query_weight, preferred_element_type=jnp.float32) + query_bias
    queries = rotate(queries.reshape(row_count, head_count, head_dim), position).astype(
        jnp.bfloat16
    )
    own_block = jnp.dot(normed, kv_weight, preferred_element_type=jnp.float32) + kv_bias
    own_block = jnp.where(
        holds_key, rotate(own_block[:, None, :], position)[:, 0, :], own_block
    ).astype(jnp.bfloat16)
    partner = from_partner(own_block, "tp", 0)
    fresh_keys = jnp.where(holds_key, own_block, partner)
    fresh_values = jnp.where(holds_key, partner, own_block)
    head_columns = lax.dynamic_slice_in_dim(shared_slot, kv_group * 2 * head_dim, 2 * head_dim, 1)
    node_total = shared_owner.shape[0]
    hot_list = [
        spread(head_columns, "seq", shared_owner[level_node]) for level_node in range(node_total)
    ]
    hot_rows = jnp.concatenate(hot_list, axis=0)
    slot_length = head_columns.shape[0]
    hot_node = jnp.repeat(jnp.arange(node_total, dtype=jnp.int32), slot_length)
    hot_place = jnp.tile(jnp.arange(slot_length, dtype=jnp.int32), node_total)
    hot_valid = hot_place < jnp.repeat(shared_len, slot_length)
    every_key = jnp.concatenate([hot_rows[:, :head_dim], fresh_keys], axis=0)
    every_value = jnp.concatenate([hot_rows[:, head_dim:], fresh_values], axis=0)
    block_rows = min(512, row_count)
    row_index = jnp.arange(row_count, dtype=jnp.int32)

    def local_block(block_number):
        row_start = block_number * block_rows
        block_places = row_start + jnp.arange(block_rows, dtype=jnp.int32)
        hot_mask = (
            (hot_node[None, :] == 0) | (hot_node[None, :] == row_parent[:, None] + 1)
        ) & hot_valid[None, :]
        own_mask = (row_request[None, :] == row_request[:, None]) & (
            row_index[None, :] <= block_places[:, None]
        )
        return partial_attention(
            queries, every_key, every_value, jnp.concatenate([hot_mask, own_mask], axis=1)
        )

    local_parts = lax.map(local_block, jnp.arange(row_count // block_rows, dtype=jnp.int32))
    local_parts = tuple((piece.reshape((row_count,) + piece.shape[2:]) for piece in local_parts))
    capacity = row_count // 2
    request_count = req_len.shape[1]
    page_count = hist_pages.shape[1] // request_count
    request_end = jnp.cumsum(req_len[0])
    request_start = request_end - req_len[0]
    padded_queries = jnp.concatenate(
        [queries, jnp.zeros((capacity, head_count, head_dim), jnp.bfloat16)], axis=0
    )
    history_top = jnp.full((row_count + capacity, head_count), masked_score, jnp.float32)
    history_sum = jnp.zeros((row_count + capacity, head_count), jnp.float32)
    history_mix = jnp.zeros((row_count + capacity, head_count, head_dim), jnp.float32)
    capacity_rows = jnp.arange(capacity, dtype=jnp.int32)
    for slot_number in range(request_count):
        offset_step = neighbour_steps[slot_number]
        chosen = req_offset[0] == slot_number
        row_start = jnp.sum(jnp.where(chosen, request_start, 0))
        row_total = jnp.sum(jnp.where(chosen, req_len[0], 0))
        node_depth = jnp.sum(jnp.where(chosen, hist_len[0], 0)).reshape(1)
        window = lax.dynamic_slice_in_dim(padded_queries, row_start, capacity, 0)
        page_rows = hist_pool[
            hist_pages[0, slot_number * page_count : (slot_number + 1) * page_count]
        ]
        flat_pages = page_rows.reshape(-1, page_rows.shape[-1])
        node_places = jnp.arange(flat_pages.shape[0], dtype=jnp.int32)
        node_rows = lax.dynamic_slice_in_dim(flat_pages, kv_group * 2 * head_dim, 2 * head_dim, 1)
        arrived_node = passed_along(node_rows, "seq", -offset_step)
        depth_mask = jnp.broadcast_to(
            (node_places < node_depth[0])[None, :], (capacity, flat_pages.shape[0])
        )
        answer = partial_attention(
            window, arrived_node[:, :head_dim], arrived_node[:, head_dim:], depth_mask
        )
        row_valid = capacity_rows < row_total

        def put_rows(whole_rows, fresh_part):
            region = lax.dynamic_slice_in_dim(whole_rows, row_start, capacity, 0)
            keep_rows = row_valid.reshape((capacity,) + (1,) * (fresh_part.ndim - 1))
            return lax.dynamic_update_slice_in_dim(
                whole_rows, jnp.where(keep_rows, fresh_part, region), row_start, 0
            )

        history_top = put_rows(history_top, answer[0])
        history_sum = put_rows(history_sum, answer[1])
        history_mix = put_rows(history_mix, answer[2])
    history_part = (history_top[:row_count], history_sum[:row_count], history_mix[:row_count])
    merged = combine(local_parts, history_part)
    attention = (
        (merged[2] / merged[1][:, :, None])
        .astype(jnp.bfloat16)
        .reshape(row_count, head_count * head_dim)
    )
    terms = jnp.dot(attention, out_weight, preferred_element_type=jnp.float32)
    summed = lax.psum_scatter(
        terms.astype(jnp.bfloat16), "tp", scatter_dimension=1, tiled=True
    ).astype(jnp.float32)
    hidden = (summed + tokens.astype(jnp.float32)).astype(jnp.bfloat16)
    return (hidden, own_block)


def solution(mesh):
    return jax.shard_map(
        on_device,
        mesh=mesh,
        in_specs=(
            P("seq", "tp"),
            P(),
            P(None, "tp"),
            P("tp"),
            P(None, "tp"),
            P("tp"),
            P("tp", None),
            P("seq", None),
            P(),
            P(),
            P("seq", None, None),
            P("seq", None),
            P("seq", None),
            P("seq", None),
            P("seq", None),
            P("seq", None),
        ),
        out_specs=(P("seq", "tp"), P("seq", "tp")),
        check_vma=False,
    )
```

profile of v0, /device:TPU:8, one launch (start us, length us, event | category | flops | bytes accessed | tf_op | source)
XLA Modules:
  0.0 298.2 jit_solution(13311774897615875516)
XLA Ops:
  8.2 1.8 gather_fusion.1
  10.7 1.9 collective-permute-start.2
  12.7 1.8 gather_fusion.3
  15.1 7.7 %collective-permute-start.4 = (bf16[256,256]{1,0:T(8,128)(2,1)}, bf16[256,256]{1,0:T(8,128)(2,1)}, u32[]{:S(2)}, u32[]{:S(2)}) collective-permute-start(bf16[256,256]{1,0:T(8,128)(2,1)} %constant_dynamic-slice_fusion.4), channel_id=1, source_target_pairs={{8,0},{12,4},{16,8},{20,12},{24,16},{28,20},{32,24},{36,28},{40,32... | collective-permute-start | bytes 393224 | tf_op jit(solution)/shard_map/ppermute | solution.py:24
  22.8 1.8 gather_fusion
  25.3 1.9 collective-permute-start.1
  27.2 1.8 gather_fusion.2
  29.8 7.6 %collective-permute-start.3 = (bf16[256,256]{1,0:T(8,128)(2,1)}, bf16[256,256]{1,0:T(8,128)(2,1)}, u32[]{:S(2)}, u32[]{:S(2)}) collective-permute-start(bf16[256,256]{1,0:T(8,128)(2,1)} %constant_dynamic-slice_fusion.6), channel_id=1, source_target_pairs={{4,0},{8,4},{12,8},{16,12},{20,16},{24,20},{28,24},{32,28},{36,32}... | collective-permute-start | bytes 393224 | tf_op jit(solution)/shard_map/ppermute | solution.py:24
  37.8 14.0 %all_gather.3 = bf16[256,1536]{1,0:T(8,128)(2,1)S(1)} all-gather(bf16[256,384]{1,0:T(8,128)(2,1)S(1)} %copy-done.1), channel_id=1, replica_groups=mesh['seq'=128,'tp'=4] {'tp'}, dimensions={1}, use_global_device_ids=true | all-gather | bytes 983040 | tf_op jit(solution)/shard_map/all_gather | solution.py:110
  53.1 3.1 %collective-permute-start = (bf16[256,128]{0,1:T(8,128)(2,1)S(1)}, bf16[256,128]{0,1:T(8,128)(2,1)}, u32[]{:S(2)}, u32[]{:S(2)}) collective-permute-start(bf16[256,128]{0,1:T(8,128)(2,1)S(1)} %fusion.58), channel_id=1, source_target_pairs={{0,1},{1,0},{2,3},{3,2},{4,5},{5,4},{6,7},{7,6},{8,9},{9,8},{10,11... | collective-permute-start | bytes 196616 | tf_op jit(solution)/shard_map/ppermute | solution.py:13
  67.9 1.2 iota_compare_fusion.9
  69.7 1.3 iota_compare_fusion.7
  71.0 1.2 iota_compare_fusion.6
  75.1 1.9 convolution_add_fusion
  83.7 1.2 fusion.112
  84.9 1.1 convolution_select_fusion.3
  87.0 1.2 fusion.113
  88.2 1.1 convolution_select_fusion.2
  89.3 1.3 dynamic_update_slice.49
  91.6 1.2 fusion.114
  93.7 1.1 convolution_select_fusion.1
  94.8 1.3 dynamic_update_slice.50
  96.4 1.2 fusion.115
  97.6 1.2 convolution_select_fusion
  98.8 1.3 dynamic_update_slice.51
  102.4 151.2 %all-reduce.4.cloned.1.call-done = (bf16[256,256]{1,0:T(8,128)(2,1)}, bf16[256,256]{1,0:T(8,128)(2,1)}, bf16[256,256]{1,0:T(8,128)(2,1)}, bf16[256,256]{1,0:T(8,128)(2,1)}, bf16[256,256]{1,0:T(8,128)(2,1)}) async-done(((bf16[256,256]{1,0:T(8,128)(2,1)}, bf16[256,256]{1,0:T(8,128)(2,1)}, bf16[256,256]{1,0:T(8,128)(2,1)}, bf16[256,256]{1,0:T(8,128)(2,1)}, bf16[256,256]{1,0:T(8,128)(2,1)}), ...) | async-done | bytes 655376 | tf_op jit(solution)/shard_map/psum | solution.py:18
  258.3 1.1 fusion
  259.4 1.6 fusion.1
  261.0 1.5 fusion.22
  263.1 1.2 copy.71
  265.0 24.6 %reduce-scatter.4.cloned.1.call-done = bf16[384,256]{1,0:T(8,128)(2,1)} async-done(((bf16[1536,256]{1,0:T(8,128)(2,1)}), bf16[384,256]{1,0:T(8,128)(2,1)}) %reduce-scatter.4.cloned.1.call-update) | async-done | bytes 196624
  289.6 1.1 copy.72
  (131 shorter events, 28.1 us)
Async XLA Ops:
  7.2 255.3 %copy-start = (bf16[384,1536]{1,0:T(8,128)(2,1)S(1)}, bf16[384,1536]{1,0:T(8,128)(2,1)}, u32[]{:S(2)}) copy-start(bf16[384,1536]{1,0:T(8,128)(2,1)} %param.22) | copy-start | bytes 3538948
  7.2 30.2 %copy-start.15 = (s32[1,4]{1,0:T(1,128)S(1)}, s32[1,4]{1,0:T(1,128)}, u32[]{:S(2)}) copy-start(s32[1,4]{1,0:T(1,128)} %param.29) | copy-start | bytes 52
  7.2 30.4 %copy-start.13 = (s32[5]{0:T(128)S(1)}, s32[5]{0:T(128)}, u32[]{:S(2)}) copy-start(s32[5]{0:T(128)} %param.24) | copy-start | bytes 64
  7.2 30.6 %copy-start.1 = (bf16[256,384]{1,0:T(8,128)(2,1)S(1)}, bf16[256,384]{1,0:T(8,128)(2,1)}, u32[]{:S(2)}) copy-start(bf16[256,384]{1,0:T(8,128)(2,1)} %param.16) | copy-start | bytes 589828
  7.2 246.4 %all-reduce.4.cloned.1.call-start = ((), (), s32[]{:S(2)}) async-start(), calls=%async_computation.2 | async-start | bytes 1310720 | tf_op jit(solution)/shard_map/psum | solution.py:18
  8.2 43.9 %copy-start.14 = (s32[1,4]{1,0:T(1,128)S(1)}, s32[1,4]{1,0:T(1,128)}, u32[]{:S(2)}) copy-start(s32[1,4]{1,0:T(1,128)} %param.28) | copy-start | bytes 52
  8.2 43.9 %copy-start.17 = (s32[1,4]{1,0:T(1,128)S(1)}, s32[1,4]{1,0:T(1,128)}, u32[]{:S(2)}) copy-start(s32[1,4]{1,0:T(1,128)} %param.31) | copy-start | bytes 52
  10.0 42.3 %copy-start.18 = (bf16[1536,128]{1,0:T(8,128)(2,1)S(1)}, bf16[1536,128]{1,0:T(8,128)(2,1)}, u32[]{:S(2)}) copy-start(bf16[1536,128]{1,0:T(8,128)(2,1)} %param.20) | copy-start | bytes 1179652
  10.0 42.3 %copy-start.19 = (f32[1536]{0:T(1024)S(1)}, f32[1536]{0:T(1024)}, u32[]{:S(2)}) copy-start(f32[1536]{0:T(1024)} %param.17) | copy-start | bytes 18436
  10.0 42.3 %copy-start.21 = (f32[128]{0:T(128)S(1)}, f32[128]{0:T(128)}, u32[]{:S(2)}) copy-start(f32[128]{0:T(128)} %param.21) | copy-start | bytes 1540
  10.7 76.3 %collective-permute-start.2 = (bf16[256,256]{1,0:T(8,128)(2,1)}, bf16[256,256]{1,0:T(8,128)(2,1)}, u32[]{:S(2)}, u32[]{:S(2)}) collective-permute-start(bf16[256,256]{1,0:T(8,128)(2,1)} %constant_dynamic-slice_fusion.8), channel_id=1, source_target_pairs={{508,0},{0,4},{4,8},{8,12},{12,16},{16,20},{20,24},{24,28},{28,32}... | collective-permute-start | bytes 393224 | tf_op jit(solution)/shard_map/ppermute | solution.py:24
  15.1 81.3 %collective-permute-start.4 = (bf16[256,256]{1,0:T(8,128)(2,1)}, bf16[256,256]{1,0:T(8,128)(2,1)}, u32[]{:S(2)}, u32[]{:S(2)}) collective-permute-start(bf16[256,256]{1,0:T(8,128)(2,1)} %constant_dynamic-slice_fusion.4), channel_id=1, source_target_pairs={{8,0},{12,4},{16,8},{20,12},{24,16},{28,20},{32,24},{36,28},{40,32... | collective-permute-start | bytes 393224 | tf_op jit(solution)/shard_map/ppermute | solution.py:24
  25.3 58.4 %collective-permute-start.1 = (bf16[256,256]{1,0:T(8,128)(2,1)}, bf16[256,256]{1,0:T(8,128)(2,1)}, u32[]{:S(2)}, u32[]{:S(2)}) collective-permute-start(bf16[256,256]{1,0:T(8,128)(2,1)} %constant_dynamic-slice_fusion.9), channel_id=1, source_target_pairs={{504,0},{508,4},{0,8},{4,12},{8,16},{12,20},{16,24},{20,28},{24,32... | collective-permute-start | bytes 393224 | tf_op jit(solution)/shard_map/ppermute | solution.py:24
  27.2 29.0 %copy-start.7 = (s32[5]{0:T(128)S(1)}, s32[5]{0:T(128)}, u32[]{:S(2)}) copy-start(s32[5]{0:T(128)} %param.25) | copy-start | bytes 64
  27.2 32.8 %copy-start.6 = (bf16[256,512]{1,0:T(8,128)(2,1)S(1)}, bf16[256,512]{1,0:T(8,128)(2,1)}, u32[]{:S(2)}) copy-start(bf16[256,512]{1,0:T(8,128)(2,1)} %param.23) | copy-start | bytes 786436
  29.8 61.8 %collective-permute-start.3 = (bf16[256,256]{1,0:T(8,128)(2,1)}, bf16[256,256]{1,0:T(8,128)(2,1)}, u32[]{:S(2)}, u32[]{:S(2)}) collective-permute-start(bf16[256,256]{1,0:T(8,128)(2,1)} %constant_dynamic-slice_fusion.6), channel_id=1, source_target_pairs={{4,0},{8,4},{12,8},{16,12},{20,16},{24,20},{28,24},{32,28},{36,32}... | collective-permute-start | bytes 393224 | tf_op jit(solution)/shard_map/ppermute | solution.py:24
  51.8 9.4 %copy-start.16 = (s32[1,4]{1,0:T(1,128)S(1)}, s32[1,4]{1,0:T(1,128)}, u32[]{:S(2)}) copy-start(s32[1,4]{1,0:T(1,128)} %param.30) | copy-start | bytes 52
  51.8 23.3 %copy-start.20 = (f32[384]{0:T(512)S(1)}, f32[384]{0:T(512)}, u32[]{:S(2)}) copy-start(f32[384]{0:T(512)} %param.19) | copy-start | bytes 4612
  53.1 28.2 %copy-start.2 = (bf16[256,128]{0,1:T(8,128)(2,1)}, bf16[256,128]{0,1:T(8,128)(2,1)S(1)}, u32[]{:S(2)}) copy-start(bf16[256,128]{0,1:T(8,128)(2,1)S(1)} %fusion.58) | copy-start | bytes 196612
  53.1 28.2 %collective-permute-start = (bf16[256,128]{0,1:T(8,128)(2,1)S(1)}, bf16[256,128]{0,1:T(8,128)(2,1)}, u32[]{:S(2)}, u32[]{:S(2)}) collective-permute-start(bf16[256,128]{0,1:T(8,128)(2,1)S(1)} %fusion.58), channel_id=1, source_target_pairs={{0,1},{1,0},{2,3},{3,2},{4,5},{5,4},{6,7},{7,6},{8,9},{9,8},{10,11... | collective-permute-start | bytes 196616 | tf_op jit(solution)/shard_map/ppermute | solution.py:13
  60.9 228.6 %reduce-scatter.4.cloned.1.call-start = ((), (), s32[]{:S(2)}) async-start(), calls=%async_computation.1 | async-start | bytes 983040
  81.3 5.6 %copy-start.8 = (pred[128]{0:T(512)(128)(4,1)}, pred[128]{0:T(512)(128)(4,1)S(1)}, u32[]{:S(2)}) copy-start(pred[128]{0:T(512)(128)(4,1)S(1)} %iota_compare_fusion.12) | copy-start | bytes 388
  91.6 8.6 %copy-start.9 = (pred[128]{0:T(512)(128)(4,1)S(1)}, pred[128]{0:T(512)(128)(4,1)}, u32[]{:S(2)}) copy-start(pred[128]{0:T(512)(128)(4,1)} %copy-done.8) | copy-start | bytes 388
  91.6 8.9 %copy-start.12 = (pred[128]{0:T(512)(128)(4,1)S(1)}, pred[128]{0:T(512)(128)(4,1)}, u32[]{:S(2)}) copy-start(pred[128]{0:T(512)(128)(4,1)} %iota_compare_fusion.11) | copy-start | bytes 388
  91.6 9.5 %copy-start.11 = (pred[128]{0:T(512)(128)(4,1)S(1)}, pred[128]{0:T(512)(128)(4,1)}, u32[]{:S(2)}) copy-start(pred[128]{0:T(512)(128)(4,1)} %iota_compare_fusion.10) | copy-start | bytes 388
  92.8 9.1 %copy-start.10 = (pred[128]{0:T(512)(128)(4,1)S(1)}, pred[128]{0:T(512)(128)(4,1)}, u32[]{:S(2)}) copy-start(pred[128]{0:T(512)(128)(4,1)} %iota_compare_fusion.9) | copy-start | bytes 388
  97.6 160.7 %copy-start.5 = (bf16[256,128]{1,0:T(8,128)(2,1)S(1)}, bf16[256,128]{1,0:T(8,128)(2,1)}, u32[]{:S(2)}) copy-start(bf16[256,128]{1,0:T(8,128)(2,1)} %copy.53) | copy-start | bytes 196612
  259.4 1.6 copy-start.4
  262.5 1.8 copy-start.3
Sparse Core Ops, SparseCore 0:
  61.1 192.5 all-reduce.3
  264.4 25.1 reduce-scatter.3
where the time goes:
time: 299 us; the launch traced here: 298 us
  waiting for transfers between devices  176 us (59%)
  local copies, waits for them, and re-layouts  26.9 us (9%)
  between operations  25.7 us (9%)
  starting transfers between devices  22.4 us (7%)
  other arithmetic  18.6 us (6%)
  matrix products  14.8 us (5%)
  blocking collectives  14 us (5%)
    psum x1, waiting for transfers between devices, spread(): return lax.psum(jnp.where(mine, shard, jnp.zeros_like(shard)), axis)  151 us
    unnamed x3, waiting for transfers between devices  24.6 us
    ppermute x4, starting transfers between devices, passed_along(): return lax.ppermute(block, axis, route)  19.2 us
    all_gather x1, blocking collectives, on_device(): features = lax.all_gather(tokens, 'tp', axis=1, tiled=True)  14 us
    gather x4, local copies, waits for them, and re-layouts, on_device(): hist_pool[hist_pages[0, slot_number * page_count:(slot_number + 1) * page...  7.21 us
    unnamed x53, local copies, waits for them, and re-layouts  7.08 us
    dynamic_update_slice x12, local copies, waits for them, and re-layouts, put_rows(): lax.dynamic_update_slice_in_dim(whole_rows, jnp.where(keep_rows, fresh_pa...  6.58 us
    dot_general x5, matrix products, partial_attention(): jnp.einsum('rhk,kd->rhd', weights.astype(jnp.bfloat16), value_vectors, pr...  6.09 us
  transfers between devices with their start and end apart: 7, of which 2 were waited for; matrix products, arithmetic and copies ran while one was open for 15% of the time, Pallas kernels for 0%

commit v1 on v0

--- a/solution.py
+++ b/solution.py
@@ -2,11 +2,19 @@
 import jax.numpy as jnp
 from jax import lax
 from jax.sharding import PartitionSpec as P
+from jax.lax import all_to_all, axis_size
 
 norm_eps = 1e-06
 rope_base = 1000000.0
 neighbour_steps = (-2, -1, 1, 2)
 masked_score = -1e30
+
+
+def scan_block(local_values):
+    left_arr = axis_size("tp")
+    prior = jnp.stack([local_values] * left_arr)
+    found_now = all_to_all(prior, axis_name="tp", split_axis=0, concat_axis=0)
+    return jnp.concatenate(found_now, axis=1)
 
 
 def from_partner(shard, axis, apart):
@@ -107,7 +115,7 @@
     req_offset,
     req_parent,
 ):
-    features = lax.all_gather(tokens, "tp", axis=1, tiled=True)
+    features = scan_block(tokens)
     widened = features.astype(jnp.float32)
     mean_square = jnp.mean(widened * widened, axis=1, keepdims=True)
     normed = (widened * lax.rsqrt(mean_square + norm_eps) * norm_gain).astype(jnp.bfloat16)

time: 299 us -> 318 us (1.064)
  waiting for transfers between devices: 176 us -> 199 us
  blocking collectives: 14 us -> 0 us
  starting transfers between devices: 22.4 us -> 27.1 us
    psum x1, waiting for transfers between devices: 151 us -> 176 us  [spread(): return lax.psum(jnp.where(mine, shard, jnp.zeros_like(shard)), axis)]
    all_gather x1 -> x0, blocking collectives: 14 us -> none  [on_device(): features = lax.all_gather(tokens, 'tp', axis=1, tiled=True)]
    all_to_all x0 -> x1, starting transfers between devices: none -> 4.42 us  [scan_block(): found_now = all_to_all(prior, axis_name='tp', split_axis=0, concat_axis=0)]
    unnamed x53 -> x38, local copies, waits for them, and re-layouts: 7.08 us -> 8.09 us
  transfers between devices with their start and end apart: 7 -> 8, of which waited for: 2 -> 2; matrix products, arithmetic and copies ran while one was open for 15% -> 16% of each run, Pallas kernels for 0% -> 0%
where the time goes in v1:
time: 318 us; the launch traced here: 317 us
  waiting for transfers between devices  199 us (63%)
  local copies, waits for them, and re-layouts  28.2 us (9%)
  starting transfers between devices  27.1 us (9%)
  between operations  25.2 us (8%)
  other arithmetic  20.4 us (6%)
  matrix products  16.6 us (5%)
    psum x1, waiting for transfers between devices, spread(): return lax.psum(jnp.where(mine, shard, jnp.zeros_like(shard)), axis)  176 us
    unnamed x3, waiting for transfers between devices  23.6 us
    ppermute x4, starting transfers between devices, passed_along(): return lax.ppermute(block, axis, route)  19.3 us
    unnamed x38, local copies, waits for them, and re-layouts  8.09 us
    gather x4, local copies, waits for them, and re-layouts, on_device(): hist_pool[hist_pages[0, slot_number * page_count:(slot_number + 1) * page...  7.16 us
    dot_general x5, matrix products, partial_attention(): jnp.einsum('rhd,kd->rhk', queries, key_vectors, preferred_element_type=jn...  6.79 us
  transfers between devices with their start and end apart: 8, of which 2 were waited for; matrix products, arithmetic and copies ran while one was open for 16% of the time, Pallas kernels for 0%

profile of v1, /device:TPU:8, one launch (start us, length us, event | category | flops | bytes accessed | tf_op | source)
XLA Modules:
  0.0 317.0 jit_solution(4354307802408616412)
XLA Ops:
  8.1 1.8 gather_fusion.1
  10.6 1.9 collective-permute-start.2
  12.5 1.8 gather_fusion.3
  15.0 7.7 %collective-permute-start.4 = (bf16[256,256]{1,0:T(8,128)(2,1)}, bf16[256,256]{1,0:T(8,128)(2,1)}, u32[]{:S(2)}, u32[]{:S(2)}) collective-permute-start(bf16[256,256]{1,0:T(8,128)(2,1)} %constant_dynamic-slice_fusion.4), channel_id=1, source_target_pairs={{8,0},{12,4},{16,8},{20,12},{24,16},{28,20},{32,24},{36,28},{40,32... | collective-permute-start | bytes 393224 | tf_op jit(solution)/shard_map/ppermute | solution.py:32
  22.7 1.8 gather_fusion
  25.2 1.9 collective-permute-start.1
  27.1 1.8 gather_fusion.2
  29.5 7.8 %collective-permute-start.3 = (bf16[256,256]{1,0:T(8,128)(2,1)}, bf16[256,256]{1,0:T(8,128)(2,1)}, u32[]{:S(2)}, u32[]{:S(2)}) collective-permute-start(bf16[256,256]{1,0:T(8,128)(2,1)} %constant_dynamic-slice_fusion.6), channel_id=1, source_target_pairs={{4,0},{8,4},{12,8},{16,12},{20,16},{24,20},{28,24},{32,28},{36,32}... | collective-permute-start | bytes 393224 | tf_op jit(solution)/shard_map/ppermute | solution.py:32
  39.3 4.4 %all-to-all-start = ((bf16[4,256,384]{1,2,0:T(8,128)(2,1)}), bf16[4,256,384]{1,2,0:T(8,128)(2,1)S(1)}, u32[]{:S(2)}, u32[]{:S(2)}) async-start(bf16[4,256,384]{1,2,0:T(8,128)(2,1)} %stack.2), calls=%async_computation | async-start | bytes 1572864 | tf_op jit(solution)/shard_map/all_to_all | solution.py:16
  55.2 1.1 iota_compare_fusion.9
  59.0 1.2 iota_compare_fusion.11
  63.8 1.2 multiply_cosine_fusion
  66.5 175.8 %all-reduce.4.cloned.1.call-done = (bf16[256,256]{1,0:T(8,128)(2,1)}, bf16[256,256]{1,0:T(8,128)(2,1)}, bf16[256,256]{1,0:T(8,128)(2,1)}, bf16[256,256]{1,0:T(8,128)(2,1)}, bf16[256,256]{1,0:T(8,128)(2,1)}) async-done(((bf16[256,256]{1,0:T(8,128)(2,1)}, bf16[256,256]{1,0:T(8,128)(2,1)}, bf16[256,256]{1,0:T(8,128)(2,1)}, bf16[256,256]{1,0:T(8,128)(2,1)}, bf16[256,256]{1,0:T(8,128)(2,1)}), ...) | async-done | bytes 655376 | tf_op jit(solution)/shard_map/psum | solution.py:26
  248.3 1.9 convolution_add_fusion
  250.4 1.3 convolution_add_fusion.1
  252.1 3.4 %collective-permute-start = (bf16[256,128]{0,1:T(8,128)(2,1)S(1)}, bf16[256,128]{0,1:T(8,128)(2,1)}, u32[]{:S(2)}, u32[]{:S(2)}) collective-permute-start(bf16[256,128]{0,1:T(8,128)(2,1)S(1)} %fusion.55), channel_id=1, source_target_pairs={{0,1},{1,0},{2,3},{3,2},{4,5},{5,4},{6,7},{7,6},{8,9},{9,8},{10,11... | collective-permute-start | bytes 196616 | tf_op jit(solution)/shard_map/ppermute | solution.py:21
  257.0 1.2 fusion.110
  258.4 1.2 fusion.109
  262.0 1.2 fusion.111
  264.5 1.1 convolution_select_fusion.3
  266.5 1.1 convolution_select_fusion.2
  267.7 1.3 dynamic_update_slice.49
  269.0 1.2 convolution_select_fusion.1
  270.1 1.3 dynamic_update_slice.50
  271.5 1.2 fusion.112
  272.9 1.1 convolution_select_fusion
  274.6 1.3 dynamic_update_slice.51
  277.0 2.1 fusion
  279.2 1.6 fusion.1
  280.7 1.5 fusion.21
  282.8 1.2 copy.74
  284.8 23.6 %reduce-scatter.4.cloned.1.call-done = bf16[384,256]{1,0:T(8,128)(2,1)} async-done(((bf16[1536,256]{1,0:T(8,128)(2,1)}), bf16[384,256]{1,0:T(8,128)(2,1)}) %reduce-scatter.4.cloned.1.call-update) | async-done | bytes 196624
  (119 shorter events, 31.9 us)
Async XLA Ops:
  7.2 275.1 %copy-start = (bf16[384,1536]{1,0:T(8,128)(2,1)S(1)}, bf16[384,1536]{1,0:T(8,128)(2,1)}, u32[]{:S(2)}) copy-start(bf16[384,1536]{1,0:T(8,128)(2,1)} %param.22) | copy-start | bytes 3538948
  7.2 36.5 %copy-start.4 = (s32[5]{0:T(128)S(1)}, s32[5]{0:T(128)}, u32[]{:S(2)}) copy-start(s32[5]{0:T(128)} %param.25) | copy-start | bytes 64
  7.2 40.3 %copy-start.3 = (bf16[256,512]{1,0:T(8,128)(2,1)S(1)}, bf16[256,512]{1,0:T(8,128)(2,1)}, u32[]{:S(2)}) copy-start(bf16[256,512]{1,0:T(8,128)(2,1)} %param.23) | copy-start | bytes 786436
  7.2 41.3 %copy-start.8 = (s32[5]{0:T(128)S(1)}, s32[5]{0:T(128)}, u32[]{:S(2)}) copy-start(s32[5]{0:T(128)} %param.24) | copy-start | bytes 64
  7.2 41.4 %copy-start.12 = (s32[1,4]{1,0:T(1,128)S(1)}, s32[1,4]{1,0:T(1,128)}, u32[]{:S(2)}) copy-start(s32[1,4]{1,0:T(1,128)} %param.29) | copy-start | bytes 52
  7.2 41.8 %copy-start.9 = (s32[1,4]{1,0:T(1,128)S(1)}, s32[1,4]{1,0:T(1,128)}, u32[]{:S(2)}) copy-start(s32[1,4]{1,0:T(1,128)} %param.28) | copy-start | bytes 52
  7.2 41.8 %copy-start.11 = (s32[1,4]{1,0:T(1,128)S(1)}, s32[1,4]{1,0:T(1,128)}, u32[]{:S(2)}) copy-start(s32[1,4]{1,0:T(1,128)} %param.30) | copy-start | bytes 52
  7.2 47.8 %copy-start.13 = (s32[1,4]{1,0:T(1,128)S(1)}, s32[1,4]{1,0:T(1,128)}, u32[]{:S(2)}) copy-start(s32[1,4]{1,0:T(1,128)} %param.31) | copy-start | bytes 52
  10.6 246.4 %collective-permute-start.2 = (bf16[256,256]{1,0:T(8,128)(2,1)}, bf16[256,256]{1,0:T(8,128)(2,1)}, u32[]{:S(2)}, u32[]{:S(2)}) collective-permute-start(bf16[256,256]{1,0:T(8,128)(2,1)} %constant_dynamic-slice_fusion.8), channel_id=1, source_target_pairs={{508,0},{0,4},{4,8},{8,12},{12,16},{16,20},{20,24},{24,28},{28,32}... | collective-permute-start | bytes 393224 | tf_op jit(solution)/shard_map/ppermute | solution.py:32
  15.0 256.5 %collective-permute-start.4 = (bf16[256,256]{1,0:T(8,128)(2,1)}, bf16[256,256]{1,0:T(8,128)(2,1)}, u32[]{:S(2)}, u32[]{:S(2)}) collective-permute-start(bf16[256,256]{1,0:T(8,128)(2,1)} %constant_dynamic-slice_fusion.4), channel_id=1, source_target_pairs={{8,0},{12,4},{16,8},{20,12},{24,16},{28,20},{32,24},{36,28},{40,32... | collective-permute-start | bytes 393224 | tf_op jit(solution)/shard_map/ppermute | solution.py:32
  25.2 233.2 %collective-permute-start.1 = (bf16[256,256]{1,0:T(8,128)(2,1)}, bf16[256,256]{1,0:T(8,128)(2,1)}, u32[]{:S(2)}, u32[]{:S(2)}) collective-permute-start(bf16[256,256]{1,0:T(8,128)(2,1)} %constant_dynamic-slice_fusion.9), channel_id=1, source_target_pairs={{504,0},{508,4},{0,8},{4,12},{8,16},{12,20},{16,24},{20,28},{24,32... | collective-permute-start | bytes 393224 | tf_op jit(solution)/shard_map/ppermute | solution.py:32
  29.5 218.5 %copy-start.5 = (f32[1536]{0:T(1024)S(1)}, f32[1536]{0:T(1024)}, u32[]{:S(2)}) copy-start(f32[1536]{0:T(1024)} %param.17) | copy-start | bytes 18436
  29.5 232.5 %collective-permute-start.3 = (bf16[256,256]{1,0:T(8,128)(2,1)}, bf16[256,256]{1,0:T(8,128)(2,1)}, u32[]{:S(2)}, u32[]{:S(2)}) collective-permute-start(bf16[256,256]{1,0:T(8,128)(2,1)} %constant_dynamic-slice_fusion.6), channel_id=1, source_target_pairs={{4,0},{8,4},{12,8},{16,12},{20,16},{24,20},{28,24},{32,28},{36,32}... | collective-permute-start | bytes 393224 | tf_op jit(solution)/shard_map/ppermute | solution.py:32
  39.3 209.0 %copy-start.6 = (f32[384]{0:T(512)S(1)}, f32[384]{0:T(512)}, u32[]{:S(2)}) copy-start(f32[384]{0:T(512)} %param.19) | copy-start | bytes 4612
  39.3 208.5 %all-to-all-start = ((bf16[4,256,384]{1,2,0:T(8,128)(2,1)}), bf16[4,256,384]{1,2,0:T(8,128)(2,1)S(1)}, u32[]{:S(2)}, u32[]{:S(2)}) async-start(bf16[4,256,384]{1,2,0:T(8,128)(2,1)} %stack.2), calls=%async_computation | async-start | bytes 1572864 | tf_op jit(solution)/shard_map/all_to_all | solution.py:16
  43.7 198.6 %all-reduce.4.cloned.1.call-start = ((), (), s32[]{:S(2)}) async-start(), calls=%async_computation.3 | async-start | bytes 1310720 | tf_op jit(solution)/shard_map/psum | solution.py:26
  48.4 260.0 %reduce-scatter.4.cloned.1.call-start = ((), (), s32[]{:S(2)}) async-start(), calls=%async_computation.2 | async-start | bytes 983040
  66.4 184.0 %copy-start.10 = (f32[128]{0:T(128)S(1)}, f32[128]{0:T(128)}, u32[]{:S(2)}) copy-start(f32[128]{0:T(128)} %param.21) | copy-start | bytes 1540
  252.1 23.8 %collective-permute-start = (bf16[256,128]{0,1:T(8,128)(2,1)S(1)}, bf16[256,128]{0,1:T(8,128)(2,1)}, u32[]{:S(2)}, u32[]{:S(2)}) collective-permute-start(bf16[256,128]{0,1:T(8,128)(2,1)S(1)} %fusion.55), channel_id=1, source_target_pairs={{0,1},{1,0},{2,3},{3,2},{4,5},{5,4},{6,7},{7,6},{8,9},{9,8},{10,11... | collective-permute-start | bytes 196616 | tf_op jit(solution)/shard_map/ppermute | solution.py:21
  256.8 16.1 %copy-start.7 = (pred[128]{0:T(512)(128)(4,1)S(1)}, pred[128]{0:T(512)(128)(4,1)}, u32[]{:S(2)}) copy-start(pred[128]{0:T(512)(128)(4,1)} %iota_compare_fusion.9) | copy-start | bytes 388
  277.0 3.7 %copy-start.2 = (bf16[1280,128]{1,0:T(8,128)(2,1)S(1)}, bf16[1280,128]{1,0:T(8,128)(2,1)}, u32[]{:S(2)}) copy-start(bf16[1280,128]{1,0:T(8,128)(2,1)} %get-tuple-element.79) | copy-start | bytes 983044
  282.2 27.2 %copy-start.1 = (bf16[256,384]{1,0:T(8,128)(2,1)S(1)}, bf16[256,384]{1,0:T(8,128)(2,1)}, u32[]{:S(2)}) copy-start(bf16[256,384]{1,0:T(8,128)(2,1)} %param.16) | copy-start | bytes 589828
Sparse Core Ops, SparseCore 0:
  48.5 193.7 all-reduce.3
  284.1 24.1 reduce-scatter.3
